TPU v7x, 256 devices: a whole 4x4x8 slice. The times are simulated.
256 devices in a mesh: loop: 16 (over z, y_lo), rep: 16 (over y_hi, x, core).
Axes of the slice: x: 4, y: 4 (y_hi: 2, y_lo: 2; y = y_hi * 2 + y_lo), z: 8, core: 2. Of those that a mesh axis runs over, the one named last changes fastest.
Arguments:
- features: bfloat16 [65536, 128], P(('loop', 'rep')), may hold values from -6 to 6
- w_self: bfloat16 [128, 256], replicated, may hold values from -0.5 to 0.5
- w_neigh: bfloat16 [128, 256], replicated, may hold values from -0.5 to 0.5
- bias: float32 [256], replicated, may hold values from -3 to 3
- degree: int32 [65536], P(('loop', 'rep')), may hold values from 1 to 4
- tiles: bfloat16 [16, 16, 16, 16, 128, 128], P('loop', 'rep'), may hold values from -0.0625 to 0.0625
- dst_block: int32 [16, 16, 16, 16], P('loop', 'rep'), may hold values from 0 to 31, as said below
- src_block: int32 [16, 16, 16, 16], P('loop', 'rep'), may hold values from 0 to 1, as said below
- live_count: int32 [16, 16, 16], P('loop', 'rep'), may hold values from 1 to 16, as said below
- cotangent: bfloat16 [65536, 256], P(('loop', 'rep')), may hold values from -6 to 6
Outputs:
- output: bfloat16 [65536, 256], P(('loop', 'rep'))
- grad_input: bfloat16 [65536, 128], P(('loop', 'rep'))
- grad_self: float32 [128, 256], replicated
- grad_neigh: float32 [128, 256], replicated
- grad_bias: float32 [256], replicated
Inputs may be any that keep to these rules, and one draw needn't show every extreme that they name: Within one (p, r, q) the 16 slots name distinct pairs (dst_block, src_block). Within one (p, r, q) the 16 slots name distinct pairs (dst_block, src_block). `live_count`: every device (p, r) has some q with all 16 slots live; slots at or past the count hold tiles that are not part of the graph.
All inputs are finite; a program needn't handle non-finite values.
Results may differ from a plain program's by a relative error of at most 0.0075.
Values may be sent and summed in bfloat16 or wider, within the bound.
A program may use at most 128 MiB of HBM per device.

v0:
```python
import math

import jax
import jax.numpy as jnp
from jax import lax
from jax.sharding import PartitionSpec as P


def shifted(block, axis, distance):
    devices = range(lax.axis_size(axis))
    route = [((i - distance) % len(devices), i) for i in devices]
    return lax.ppermute(block, axis, route)


def per_device(
    features, w_self, w_neigh, bias, degree, tiles, dst_block, src_block, live_count, cotangent
):
    loop_count = lax.axis_size("loop")
    rep_count = lax.axis_size("rep")
    loop_here = lax.axis_index("loop")
    row_count, feat_width = features.shape
    tile_size = tiles.shape[-1]
    slot_count = tiles.shape[3]
    sub_blocks = row_count // tile_size
    row_blocks = sub_blocks * rep_count
    tile_all = tiles[0, 0]
    dst_all = dst_block[0, 0]
    src_all = src_block[0, 0]
    live_all = jnp.arange(slot_count)[None, :] < live_count[0, 0][:, None]
    place_all = (
        (dst_all[:, :, None] == jnp.arange(row_blocks)[None, None, :]) & live_all[:, :, None]
    ).astype(jnp.float32)
    land_all = (
        (src_all[:, :, None] == jnp.arange(sub_blocks)[None, None, :]) & live_all[:, :, None]
    ).astype(jnp.float32)

    def pick_entry(table, source):
        return lax.dynamic_index_in_dim(table, source, 0, keepdims=False)

    def gather_term(source, panel):
        tile_part = pick_entry(tile_all, source)
        chosen = jnp.take(
            panel.reshape(sub_blocks, tile_size, feat_width), pick_entry(src_all, source), axis=0
        )
        product = jnp.einsum("tij,tjf->tif", tile_part, chosen, preferred_element_type=jnp.float32)
        return jnp.einsum(
            "td,tif->dif", pick_entry(place_all, source), product, precision=lax.Precision.HIGHEST
        )

    running = gather_term(loop_here, features)

    def one_way(step_index, state):
        panel, total = state
        panel = shifted(panel, "loop", 1)
        return (panel, total + gather_term((loop_here - step_index) % loop_count, panel))

    _, running = lax.fori_loop(1, loop_count, one_way, (features, running))
    agg_sum = lax.psum_scatter(
        running.reshape(row_blocks * tile_size, feat_width), "rep", scatter_dimension=0, tiled=True
    )
    degree_f = degree.astype(jnp.float32)[:, None]
    aggregate = (agg_sum / degree_f).astype(jnp.bfloat16)
    preact = (
        jnp.dot(features, w_self, preferred_element_type=jnp.float32)
        + jnp.dot(aggregate, w_neigh, preferred_element_type=jnp.float32)
        + bias
    )
    sigmoid_val = jax.nn.sigmoid(preact)
    output = (preact * sigmoid_val).astype(jnp.bfloat16)
    grad_pre = (
        cotangent.astype(jnp.float32) * sigmoid_val * (1.0 + preact * (1.0 - sigmoid_val))
    ).astype(jnp.bfloat16)
    grad_agg = (
        jnp.einsum("nh,fh->nf", grad_pre, w_neigh, preferred_element_type=jnp.float32) / degree_f
    ).astype(jnp.bfloat16)
    grad_whole = lax.all_gather(grad_agg, "rep", axis=0, tiled=True).reshape(
        row_blocks, tile_size, feat_width
    )
    node_total = row_count * loop_count * rep_count
    grad_scale = 1.0 / math.sqrt(node_total)
    grad_self, grad_neigh, grad_bias = lax.psum(
        (
            jnp.einsum("nf,nh->fh", features, grad_pre, preferred_element_type=jnp.float32)
            * grad_scale,
            jnp.einsum("nf,nh->fh", aggregate, grad_pre, preferred_element_type=jnp.float32)
            * grad_scale,
            jnp.sum(grad_pre.astype(jnp.float32), axis=0) * grad_scale,
        ),
        ("loop", "rep"),
    )
    self_grad = jnp.einsum("nh,fh->nf", grad_pre, w_self, preferred_element_type=jnp.float32)

    def spread_term(source):
        tile_part = pick_entry(tile_all, source)
        chosen = jnp.take(grad_whole, pick_entry(dst_all, source), axis=0)
        product = jnp.einsum("tij,tif->tjf", tile_part, chosen, preferred_element_type=jnp.float32)
        summed = jnp.einsum(
            "ts,tjf->sjf", pick_entry(land_all, source), product, precision=lax.Precision.HIGHEST
        )
        return summed.reshape(row_count, feat_width)

    def carry_along(step_index, total):
        total = shifted(total, "loop", -1)
        return total + spread_term((loop_here + 1 + step_index) % loop_count)

    neigh_grad = lax.fori_loop(
        1, loop_count, carry_along, spread_term((loop_here + 1) % loop_count)
    )
    grad_input = (self_grad + neigh_grad).astype(jnp.bfloat16)
    return (output, grad_input, grad_self, grad_neigh, grad_bias)


def solution(mesh):
    in_specs = (
        P(("loop", "rep"), None),
        P(),
        P(),
        P(),
        P(("loop", "rep")),
        P("loop", "rep", None, None, None, None),
        P("loop", "rep", None, None),
        P("loop", "rep", None, None),
        P("loop", "rep", None),
        P(("loop", "rep"), None),
    )
    out_specs = (P(("loop", "rep"), None), P(("loop", "rep"), None), P(), P(), P())
    return jax.shard_map(
        per_device, mesh=mesh, in_specs=in_specs, out_specs=out_specs, check_vma=False
    )
```

profile of v0, /device:TPU:2, one launch (start us, length us, event | category | flops | bytes accessed | tf_op | source)
XLA Modules:
  0.0 704.0 jit_solution(3189512164626604518)
XLA Ops:
  14.8 174.0 %while.32 = (s32[]{:T(128)}, bf16[256,128]{1,0:T(8,128)(2,1)S(1)}, f32[32,128,128]{2,0,1:T(8,128)S(1)}, s32[]{:T(128)}, f32[16,16,32]{2,1,0:T(8,128)S(1)}, /*ind...) while((s32[]{:T(128)}, bf16[256,128]{1,0:T(8,128)(2,1)S(1)}, ...), condition=%wide.region_1.3_spmd, body=%wide.region_0.2_spmd.sunk | while | flops 168559728 | bytes 8794716 | solution.py:57
  16.5 7.5 %collective-permute-done = bf16[256,128]{1,0:T(8,128)(2,1)S(1)} collective-permute-done((bf16[256,128]{1,0:T(8,128)(2,1)S(1)}, bf16[256,128]{1,0:T(8,128)(2,1)S(1)}, u32[]{:S(2)}, u32[]{:S(2)}) %collective-permute-start) | collective-permute-done | bytes 65568 | tf_op jit(solution)/shard_map/while/body/eval_jaxpr/ppermute | solution.py:12
  26.1 2.8 convolution_add_fusion.4
  29.1 6.3 collective-permute-done
  37.5 2.8 convolution_add_fusion.4
  40.5 6.3 collective-permute-done
  48.8 2.8 convolution_add_fusion.4
  51.8 6.3 collective-permute-done
  60.2 2.8 convolution_add_fusion.4
  63.2 6.3 collective-permute-done
  74.6 6.3 collective-permute-done
  83.0 2.8 convolution_add_fusion.4
  86.0 6.3 collective-permute-done
  94.4 2.8 convolution_add_fusion.4
  97.4 6.3 collective-permute-done
  105.8 2.8 convolution_add_fusion.4
  108.8 6.8 collective-permute-done
  117.7 2.8 convolution_add_fusion.4
  120.7 6.3 collective-permute-done
  132.0 6.3 collective-permute-done
  143.4 6.3 collective-permute-done
  151.8 2.8 convolution_add_fusion.4
  154.8 6.3 collective-permute-done
  163.2 2.8 convolution_add_fusion.4
  166.2 6.3 collective-permute-done
  174.6 2.8 convolution_add_fusion.4
  177.6 6.3 collective-permute-done
  186.0 2.8 convolution_add_fusion.4
  192.4 77.7 %reduce-scatter.2.cloned.1.call-done = f32[256,128]{1,0:T(8,128)} async-done(((f32[4096,128]{1,0:T(8,128)}), f32[256,128]{1,0:T(8,128)}) %reduce-scatter.2.cloned.1.call-update) | async-done | bytes 131088 | tf_op jit(solution)/shard_map/reduce_scatter | solution.py:58
  275.6 74.1 %psum.23 = f32[256]{0:T(256)} all-reduce(f32[256]{0:T(256)S(1)} %broadcast_multiply_fusion), channel_id=1, replica_groups=mesh['loop'=16,'rep'=16] {'loop','rep'}, use_global_device_ids=true, to_apply=%region_8.11 | all-reduce | flops 256 | bytes 2048 | tf_op jit(solution)/shard_map/psum | solution.py:81
  349.7 177.0 %all-reduce.3.cloned.1.call-done = (f32[128,256]{0,1:T(8,128)}, f32[128,256]{1,0:T(8,128)}) async-done(((f32[128,256]{0,1:T(8,128)}, f32[128,256]{1,0:T(8,128)}), (f32[128,256]{0,1:T(8,128)}, f32[128,256]{1,0:T(8,128)})) %all-reduce.3.cloned.1.call-update) | async-done | bytes 262160 | tf_op jit(solution)/shard_map/psum | solution.py:81
  528.4 50.3 %all-gather.2.cloned.1.call-done = bf16[4096,128]{1,0:T(8,128)(2,1)} async-done(((bf16[256,128]{1,0:T(8,128)(2,1)}), bf16[4096,128]{1,0:T(8,128)(2,1)}) %all-gather.2.cloned.1.call-update) | async-done | bytes 1048592 | tf_op jit(solution)/shard_map/all_gather | solution.py:76
  583.2 112.8 %while.33 = (s32[]{:T(128)}, f32[256,128]{1,0:T(8,128)S(1)}, s32[]{:T(128)}, f32[16,16,2]{1,2,0:T(2,128)S(1)}, bf16[16,16,128,128]{3,2,1,0:T(8,128)(2,1)}, /*ind...) while((s32[]{:T(128)}, f32[256,128]{1,0:T(8,128)S(1)}, ...), condition=%wide.region_4.7_spmd, body=%wide.region_3.6_spmd.sunk | while | flops 73696368 | bytes 5510748 | solution.py:106
  583.2 3.4 collective-permute-start.1
  590.6 3.8 collective-permute-start.1
  598.5 3.1 collective-permute-start.1
  605.7 3.1 collective-permute-start.1
  612.9 3.1 collective-permute-start.1
  620.1 3.5 collective-permute-start.1
  627.6 4.5 collective-permute-start.1
  636.1 3.6 collective-permute-start.1
  643.7 3.1 collective-permute-start.1
  650.9 3.1 collective-permute-start.1
  658.1 3.1 collective-permute-start.1
  665.3 3.8 collective-permute-start.1
  673.1 4.2 collective-permute-start.1
  681.3 3.4 collective-permute-start.1
  688.8 3.1 collective-permute-start.1
  (265 shorter events, 126.6 us)
Async XLA Ops:
  7.2 262.9 %copy-start = (bf16[128,256]{1,0:T(8,128)(2,1)S(1)}, bf16[128,256]{1,0:T(8,128)(2,1)}, u32[]{:S(2)}) copy-start(bf16[128,256]{1,0:T(8,128)(2,1)} %param.20) | copy-start | bytes 196612
  7.2 262.9 %reduce-scatter.2.cloned.1.call-start = ((), (), s32[]{:S(2)}) async-start(), calls=%async_computation.1 | async-start | bytes 2228224 | tf_op jit(solution)/shard_map/reduce_scatter | solution.py:58
  13.3 1.5 copy-start.5
  14.8 9.2 %collective-permute-start = (bf16[256,128]{1,0:T(8,128)(2,1)S(1)}, bf16[256,128]{1,0:T(8,128)(2,1)S(1)}, u32[]{:S(2)}, u32[]{:S(2)}) collective-permute-start(bf16[256,128]{1,0:T(8,128)(2,1)S(1)} %get-tuple-element.526), channel_id=1, source_target_pairs={{240,0},{0,16},{16,32},{32,48},{48,64},{64,80},{80,96},{96,112},{1... | collective-permute-start | bytes 196616 | tf_op jit(solution)/shard_map/while/body/eval_jaxpr/ppermute | solution.py:12
  28.9 6.5 collective-permute-start
  40.3 6.5 collective-permute-start
  51.7 6.5 collective-permute-start
  63.1 6.5 collective-permute-start
  74.5 6.5 collective-permute-start
  85.8 6.5 collective-permute-start
  97.2 6.5 collective-permute-start
  108.6 7.0 collective-permute-start
  120.5 6.5 collective-permute-start
  131.9 6.5 collective-permute-start
  143.3 6.5 collective-permute-start
  154.7 6.5 collective-permute-start
  166.1 6.5 collective-permute-start
  177.4 6.5 collective-permute-start
  191.4 0.7 copy-start.6
  191.4 0.9 copy-start.2
  191.4 0.9 copy-start.3
  191.4 78.7 %copy-start.7 = (bf16[256,256]{1,0:T(8,128)(2,1)S(1)}, bf16[256,256]{1,0:T(8,128)(2,1)}, u32[]{:S(2)}) copy-start(bf16[256,256]{1,0:T(8,128)(2,1)} %param.27) | copy-start | bytes 393220
  191.4 78.7 %copy-start.9 = (f32[256]{0:T(256)S(1)}, f32[256]{0:T(256)}, u32[]{:S(2)}) copy-start(f32[256]{0:T(256)} %param.21) | copy-start | bytes 3076
  191.4 335.3 %all-reduce.3.cloned.1.call-start = ((), (), s32[]{:S(2)}) async-start(), calls=%async_computation.3 | async-start | bytes 524288 | tf_op jit(solution)/shard_map/psum | solution.py:81
  270.1 2.9 copy-start.8
  273.9 304.7 %all-gather.2.cloned.1.call-start = ((), (), s32[]{:S(2)}) async-start(), calls=%async_computation.2 | async-start | bytes 1114112 | tf_op jit(solution)/shard_map/all_gather | solution.py:76
  578.6 4.5 copy-start.1
  583.2 113.6 %copy-start.4 = (f32[128,256]{1,0:T(8,128)S(1)}, f32[128,256]{1,0:T(8,128)}, u32[]{:S(2)}) copy-start(f32[128,256]{1,0:T(8,128)} %get-tuple-element.583) | copy-start | bytes 393220
  583.2 7.4 %collective-permute-start.1 = (f32[256,128]{1,0:T(8,128)S(1)}, f32[256,128]{1,0:T(8,128)S(1)}, u32[]{:S(2)}, u32[]{:S(2)}) collective-permute-start(f32[256,128]{1,0:T(8,128)S(1)} %get-tuple-element.559), channel_id=1, source_target_pairs={{16,0},{32,16},{48,32},{64,48},{80,64},{96,80},{112,96},{128,112},... | collective-permute-start | bytes 393224 | tf_op jit(solution)/shard_map/while/body/eval_jaxpr/ppermute | solution.py:12
  590.6 7.8 %collective-permute-start.1 = (f32[256,128]{1,0:T(8,128)S(1)}, f32[256,128]{1,0:T(8,128)S(1)}, u32[]{:S(2)}, u32[]{:S(2)}) collective-permute-start(f32[256,128]{1,0:T(8,128)S(1)} %get-tuple-element.559), channel_id=1, source_target_pairs={{16,0},{32,16},{48,32},{64,48},{80,64},{96,80},{112,96},{128,112},... | collective-permute-start | bytes 393224 | tf_op jit(solution)/shard_map/while/body/eval_jaxpr/ppermute | solution.py:12
  598.5 7.1 %collective-permute-start.1 = (f32[256,128]{1,0:T(8,128)S(1)}, f32[256,128]{1,0:T(8,128)S(1)}, u32[]{:S(2)}, u32[]{:S(2)}) collective-permute-start(f32[256,128]{1,0:T(8,128)S(1)} %get-tuple-element.559), channel_id=1, source_target_pairs={{16,0},{32,16},{48,32},{64,48},{80,64},{96,80},{112,96},{128,112},... | collective-permute-start | bytes 393224 | tf_op jit(solution)/shard_map/while/body/eval_jaxpr/ppermute | solution.py:12
  605.7 7.1 %collective-permute-start.1 = (f32[256,128]{1,0:T(8,128)S(1)}, f32[256,128]{1,0:T(8,128)S(1)}, u32[]{:S(2)}, u32[]{:S(2)}) collective-permute-start(f32[256,128]{1,0:T(8,128)S(1)} %get-tuple-element.559), channel_id=1, source_target_pairs={{16,0},{32,16},{48,32},{64,48},{80,64},{96,80},{112,96},{128,112},... | collective-permute-start | bytes 393224 | tf_op jit(solution)/shard_map/while/body/eval_jaxpr/ppermute | solution.py:12
  612.9 7.1 %collective-permute-start.1 = (f32[256,128]{1,0:T(8,128)S(1)}, f32[256,128]{1,0:T(8,128)S(1)}, u32[]{:S(2)}, u32[]{:S(2)}) collective-permute-start(f32[256,128]{1,0:T(8,128)S(1)} %get-tuple-element.559), channel_id=1, source_target_pairs={{16,0},{32,16},{48,32},{64,48},{80,64},{96,80},{112,96},{128,112},... | collective-permute-start | bytes 393224 | tf_op jit(solution)/shard_map/while/body/eval_jaxpr/ppermute | solution.py:12
  620.1 7.5 %collective-permute-start.1 = (f32[256,128]{1,0:T(8,128)S(1)}, f32[256,128]{1,0:T(8,128)S(1)}, u32[]{:S(2)}, u32[]{:S(2)}) collective-permute-start(f32[256,128]{1,0:T(8,128)S(1)} %get-tuple-element.559), channel_id=1, source_target_pairs={{16,0},{32,16},{48,32},{64,48},{80,64},{96,80},{112,96},{128,112},... | collective-permute-start | bytes 393224 | tf_op jit(solution)/shard_map/while/body/eval_jaxpr/ppermute | solution.py:12
  627.6 8.5 %collective-permute-start.1 = (f32[256,128]{1,0:T(8,128)S(1)}, f32[256,128]{1,0:T(8,128)S(1)}, u32[]{:S(2)}, u32[]{:S(2)}) collective-permute-start(f32[256,128]{1,0:T(8,128)S(1)} %get-tuple-element.559), channel_id=1, source_target_pairs={{16,0},{32,16},{48,32},{64,48},{80,64},{96,80},{112,96},{128,112},... | collective-permute-start | bytes 393224 | tf_op jit(solution)/shard_map/while/body/eval_jaxpr/ppermute | solution.py:12
  636.1 7.6 %collective-permute-start.1 = (f32[256,128]{1,0:T(8,128)S(1)}, f32[256,128]{1,0:T(8,128)S(1)}, u32[]{:S(2)}, u32[]{:S(2)}) collective-permute-start(f32[256,128]{1,0:T(8,128)S(1)} %get-tuple-element.559), channel_id=1, source_target_pairs={{16,0},{32,16},{48,32},{64,48},{80,64},{96,80},{112,96},{128,112},... | collective-permute-start | bytes 393224 | tf_op jit(solution)/shard_map/while/body/eval_jaxpr/ppermute | solution.py:12
  643.7 7.1 %collective-permute-start.1 = (f32[256,128]{1,0:T(8,128)S(1)}, f32[256,128]{1,0:T(8,128)S(1)}, u32[]{:S(2)}, u32[]{:S(2)}) collective-permute-start(f32[256,128]{1,0:T(8,128)S(1)} %get-tuple-element.559), channel_id=1, source_target_pairs={{16,0},{32,16},{48,32},{64,48},{80,64},{96,80},{112,96},{128,112},... | collective-permute-start | bytes 393224 | tf_op jit(solution)/shard_map/while/body/eval_jaxpr/ppermute | solution.py:12
  650.9 7.1 %collective-permute-start.1 = (f32[256,128]{1,0:T(8,128)S(1)}, f32[256,128]{1,0:T(8,128)S(1)}, u32[]{:S(2)}, u32[]{:S(2)}) collective-permute-start(f32[256,128]{1,0:T(8,128)S(1)} %get-tuple-element.559), channel_id=1, source_target_pairs={{16,0},{32,16},{48,32},{64,48},{80,64},{96,80},{112,96},{128,112},... | collective-permute-start | bytes 393224 | tf_op jit(solution)/shard_map/while/body/eval_jaxpr/ppermute | solution.py:12
  658.1 7.1 %collective-permute-start.1 = (f32[256,128]{1,0:T(8,128)S(1)}, f32[256,128]{1,0:T(8,128)S(1)}, u32[]{:S(2)}, u32[]{:S(2)}) collective-permute-start(f32[256,128]{1,0:T(8,128)S(1)} %get-tuple-element.559), channel_id=1, source_target_pairs={{16,0},{32,16},{48,32},{64,48},{80,64},{96,80},{112,96},{128,112},... | collective-permute-start | bytes 393224 | tf_op jit(solution)/shard_map/while/body/eval_jaxpr/ppermute | solution.py:12
  665.3 7.8 %collective-permute-start.1 = (f32[256,128]{1,0:T(8,128)S(1)}, f32[256,128]{1,0:T(8,128)S(1)}, u32[]{:S(2)}, u32[]{:S(2)}) collective-permute-start(f32[256,128]{1,0:T(8,128)S(1)} %get-tuple-element.559), channel_id=1, source_target_pairs={{16,0},{32,16},{48,32},{64,48},{80,64},{96,80},{112,96},{128,112},... | collective-permute-start | bytes 393224 | tf_op jit(solution)/shard_map/while/body/eval_jaxpr/ppermute | solution.py:12
  673.1 8.2 %collective-permute-start.1 = (f32[256,128]{1,0:T(8,128)S(1)}, f32[256,128]{1,0:T(8,128)S(1)}, u32[]{:S(2)}, u32[]{:S(2)}) collective-permute-start(f32[256,128]{1,0:T(8,128)S(1)} %get-tuple-element.559), channel_id=1, source_target_pairs={{16,0},{32,16},{48,32},{64,48},{80,64},{96,80},{112,96},{128,112},... | collective-permute-start | bytes 393224 | tf_op jit(solution)/shard_map/while/body/eval_jaxpr/ppermute | solution.py:12
  681.3 7.4 %collective-permute-start.1 = (f32[256,128]{1,0:T(8,128)S(1)}, f32[256,128]{1,0:T(8,128)S(1)}, u32[]{:S(2)}, u32[]{:S(2)}) collective-permute-start(f32[256,128]{1,0:T(8,128)S(1)} %get-tuple-element.559), channel_id=1, source_target_pairs={{16,0},{32,16},{48,32},{64,48},{80,64},{96,80},{112,96},{128,112},... | collective-permute-start | bytes 393224 | tf_op jit(solution)/shard_map/while/body/eval_jaxpr/ppermute | solution.py:12
  688.8 7.1 %collective-permute-start.1 = (f32[256,128]{1,0:T(8,128)S(1)}, f32[256,128]{1,0:T(8,128)S(1)}, u32[]{:S(2)}, u32[]{:S(2)}) collective-permute-start(f32[256,128]{1,0:T(8,128)S(1)} %get-tuple-element.559), channel_id=1, source_target_pairs={{16,0},{32,16},{48,32},{64,48},{80,64},{96,80},{112,96},{128,112},... | collective-permute-start | bytes 393224 | tf_op jit(solution)/shard_map/while/body/eval_jaxpr/ppermute | solution.py:12
Sparse Core Ops, SparseCore 0:
  191.5 78.5 reduce-scatter.1
  276.3 250.3 all-reduce.2
  530.0 48.5 all-gather.1
where the time goes:
time: 706 us; the launch traced here: 704 us
  waiting for transfers between devices  401 us (57%)
  matrix products  114 us (16%)
  blocking collectives  74.1 us (10%)
  starting transfers between devices  55.1 us (8%)
  local copies, waits for them, and re-layouts  29.7 us (4%)
  other arithmetic  14.1 us (2%)
  between operations  13.9 us (2%)
    psum x1, waiting for transfers between devices, per_device(): lax.psum((jnp.einsum('nf,nh->fh', features, grad_pre, preferred_element_t...  177 us
    ppermute x30, waiting for transfers between devices, shifted(): return lax.ppermute(block, axis, route)  96.3 us
    reduce_scatter x1, waiting for transfers between devices, per_device(): lax.psum_scatter(running.reshape(row_blocks * tile_size, feat_width), 're...  77.7 us
    psum x1, blocking collectives, per_device(): lax.psum((jnp.einsum('nf,nh->fh', features, grad_pre, preferred_element_t...  74.1 us
    ppermute x30, starting transfers between devices, shifted(): return lax.ppermute(block, axis, route)  55 us
    all_gather x1, waiting for transfers between devices, per_device(): lax.all_gather(grad_agg, 'rep', axis=0, tiled=True)  50.3 us
    dot_general x16, matrix products, gather_term(): jnp.einsum('td,tif->dif', pick_entry(place_all, source), product, precisi...  43.8 us
    dot_general x16, matrix products, spread_term(): jnp.einsum('tij,tif->tjf', tile_part, chosen, preferred_element_type=jnp....  22.8 us
  transfers between devices with their start and end apart: 33, of which 18 were waited for; matrix products, arithmetic and copies ran while one was open for 9% of the time, Pallas kernels for 0%

commit v1 on v0

v1 whole, which is shorter than its diff:
```python
import math

import jax
import jax.numpy as jnp
from jax import lax
from jax.experimental import pallas as pl
from jax.experimental.pallas import tpu as pltpu
from jax.sharding import PartitionSpec as P

F32 = jnp.float32
BF16 = jnp.bfloat16
MESH = pl.DeviceIdType.MESH
Z = 8
X = 4
CHIP_STEPS = ((1, 2), (1, 1), (1, 3), (0, 2), (1, 0), (0, 1), (0, 3))


def remote(src, dst, send_sem, recv_sem, device):
    return pltpu.make_async_remote_copy(
        src_ref=src,
        dst_ref=dst,
        send_sem=send_sem,
        recv_sem=recv_sem,
        device_id=device,
        device_id_type=MESH,
    )


def loop_node(dz, col):
    here = lax.axis_index("loop")
    z = lax.rem(here // 2 + (dz + Z), Z)
    return z * 2 + lax.rem(here % 2 + col, 2)


def chip_node(dy, dx):
    chip = lax.axis_index("rep") // 2
    return lax.rem(chip // X + dy, 2) * X + lax.rem(chip % X + dx, X)


def gather_kernel(x_ref, g_ref, own_sem, pair_sem, send_sem, recv_sem):
    rep = lax.axis_index("rep")
    half = x_ref.shape[0] // 2
    barrier = pltpu.get_barrier_semaphore()
    for dz, col in ((1, 0), (-1, 0), (0, 1)):
        pl.semaphore_signal(
            barrier, inc=1, device_id=(loop_node(dz, col), rep), device_id_type=MESH
        )
    pl.semaphore_wait(barrier, 3)
    own = pltpu.make_async_copy(x_ref, g_ref.at[loop_node(0, 0)], own_sem)
    own.start()

    def hop(way, col, k):
        sign = 1 - 2 * way
        origin = loop_node(-sign * (k - 1), col)
        src = x_ref if (k == 1 and col == 0) else g_ref.at[origin]
        dst = g_ref.at[origin]
        if k == Z // 2:
            rows = pl.ds(way * half, half)
            src, dst = src.at[rows], dst.at[rows]
        return remote(
            src,
            dst,
            send_sem.at[way, col, k - 1],
            recv_sem.at[way, col, k - 1],
            (loop_node(sign, 0), rep),
        )

    def arrival(way, col, k):
        sign = 1 - 2 * way
        dst = g_ref.at[loop_node(-sign * k, col)]
        if k == Z // 2:
            dst = dst.at[pl.ds(way * half, half)]
        return remote(
            dst,
            dst,
            send_sem.at[way, col, k - 1],
            recv_sem.at[way, col, k - 1],
            (loop_node(sign, 0), rep),
        )

    pair = remote(
        x_ref, g_ref.at[loop_node(0, 0)], pair_sem.at[0], pair_sem.at[1], (loop_node(0, 1), rep)
    )
    pair.start()
    sent = []

    def send(way, col, k):
        copy = hop(way, col, k)
        copy.start()
        sent.append(copy)

    send(0, 0, 1)
    send(1, 0, 1)
    pair_in = remote(
        x_ref, g_ref.at[loop_node(0, 1)], pair_sem.at[0], pair_sem.at[1], (loop_node(0, 1), rep)
    )
    pair_in.wait_recv()
    send(0, 1, 1)
    send(1, 1, 1)
    for k in range(1, Z // 2):
        for col in (0, 1):
            for way in (0, 1):
                arrival(way, col, k).wait_recv()
                send(way, col, k + 1)
    for col in (0, 1):
        for way in (0, 1):
            arrival(way, col, Z // 2).wait_recv()
    pair.wait_send()
    for copy in sent:
        copy.wait_send()
    own.wait()


def product_kernel(dst_ref, src_ref, live_ref, g_ref, tile_ref, out_ref, tile_vmem, acc, sems):
    sources, depth, width = tile_ref.shape
    blk = width
    slots = depth // blk
    blocks = acc.shape[0] - 1

    def fetch(q):
        return pltpu.make_async_copy(tile_ref.at[q], tile_vmem.at[q], sems.at[q])

    for q in range(sources):
        fetch(q).start()
    acc[...] = jnp.zeros_like(acc)

    def body(q, carry):
        fetch(q).wait()
        live = live_ref[q]
        for t in range(slots):
            row = jnp.where(t < live, dst_ref[q, t], blocks)
            start = pl.multiple_of(src_ref[q, t] * blk, blk)
            acc[row] += jnp.dot(
                tile_vmem[q, t * blk : (t + 1) * blk, :],
                g_ref[q, pl.ds(start, blk), :],
                preferred_element_type=F32,
            )
        return carry

    lax.fori_loop(0, sources, body, 0)
    for d in range(blocks):
        half, rep = d % 2, d // 2
        out_ref[rep % 2, rep // 2, half * blk : (half + 1) * blk, :] = acc[d].astype(BF16)


def layer_kernel(
    dst_ref,
    src_ref,
    live_ref,
    part_ref,
    x_ref,
    ws_ref,
    wn_ref,
    bias_ref,
    deg_ref,
    cot_ref,
    tile_ref,
    out_ref,
    gin_ref,
    gs_ref,
    gn_ref,
    gb_ref,
    tile_vmem,
    core_in,
    chip_out,
    chip_in,
    gt,
    lhs,
    term,
    base,
    self_grad,
    ring_out,
    ring_in,
    col_out,
    col_in,
    wpart,
    win,
    rows_out,
    rows_in,
    rows_all,
    wfull,
    tile_sem,
    core_sem,
    chip_sem,
    gath_sem,
    fwd_sem,
    ring_sem,
    col_sem,
    w1_sem,
    w2_sem,
    w3_sem,
    w4_sem,
):
    loop = lax.axis_index("loop")
    rep = lax.axis_index("rep")
    core = rep % 2
    chip = rep // 2
    mate = (loop, chip * 2 + (1 - core))
    sources, depth, blk = tile_ref.shape
    slots = depth // blk
    blocks = gt.shape[0] - 1
    peers = 16

    barrier = pltpu.get_barrier_semaphore()

    def greet(j, carry):
        pl.semaphore_signal(
            barrier, inc=1, device_id=(loop, lax.rem(rep + j, peers)), device_id_type=MESH
        )
        pl.semaphore_signal(
            barrier, inc=1, device_id=(lax.rem(loop + j, peers), rep), device_id_type=MESH
        )
        return carry

    lax.fori_loop(1, peers, greet, 0)

    def fetch(q):
        return pltpu.make_async_copy(tile_ref.at[q], tile_vmem.at[q], tile_sem.at[q])

    for q in range(sources):
        fetch(q).start()
    base[...] = (
        jnp.dot(x_ref[...], ws_ref[...], preferred_element_type=F32) + bias_ref[...]
    )
    gt[blocks] = jnp.zeros(gt.shape[1:], BF16)
    pl.semaphore_wait(barrier, 2 * (peers - 1))

    steps = CHIP_STEPS + ((0, 0),)

    def core_copy(i):
        return remote(
            part_ref.at[1 - core, chip_node(*steps[i])],
            core_in.at[i],
            core_sem.at[0, i],
            core_sem.at[1, i],
            mate,
        )

    def chip_copy(i):
        return remote(
            chip_out.at[i],
            chip_in.at[i],
            chip_sem.at[0, i],
            chip_sem.at[1, i],
            (loop, chip_node(*steps[i]) * 2 + core),
        )

    for i in range(len(steps)):
        core_copy(i).start()
    for i in range(len(steps) - 1):
        core_copy(i).wait_recv()
        both = part_ref[core, chip_node(*steps[i])].astype(F32) + core_in[i].astype(F32)
        chip_out[i] = both.astype(BF16)
        if i > 0:
            chip_copy(i - 1).start()
    last = len(steps) - 1
    core_copy(last).wait_recv()
    total = part_ref[core, chip].astype(F32) + core_in[last].astype(F32)
    chip_copy(last - 1).start()
    for i in reversed(range(last)):
        chip_copy(i).wait_recv()
        total = total + chip_in[i].astype(F32)

    deg_rows = deg_ref[...].astype(F32)
    deg_cols = jnp.concatenate(
        [
            jnp.transpose(jnp.broadcast_to(deg_rows[s : s + 1, :], (blk, blk)))
            for s in range(2)
        ],
        axis=0,
    )
    aggregate = (total / deg_cols).astype(BF16)
    preact = base[...] + jnp.dot(aggregate, wn_ref[...], preferred_element_type=F32)
    sigmoid_val = jax.nn.sigmoid(preact)
    grad_pre = (
        cot_ref[...].astype(F32) * sigmoid_val * (1.0 + preact * (1.0 - sigmoid_val))
    ).astype(BF16)
    out_ref[...] = (preact * sigmoid_val).astype(BF16)
    back = lax.dot_general(
        wn_ref[...], grad_pre, (((1,), (1,)), ((), ())), preferred_element_type=F32
    )
    for s in range(2):
        gt[rep * 2 + s] = (back[:, s * blk : (s + 1) * blk] / deg_rows[s : s + 1, :]).astype(BF16)
    self_grad[...] = lax.dot_general(
        grad_pre, ws_ref[...], (((1,), (1,)), ((), ())), preferred_element_type=F32
    )

    def gather_copy(i):
        dy, dx = CHIP_STEPS[i]
        mine = gt.at[pl.ds(rep * 2, 2)]
        return remote(
            mine,
            mine,
            gath_sem.at[0, i],
            gath_sem.at[1, i],
            (loop, chip_node(dy, dx) * 2 + core),
        )

    def gathered(i):
        dy, dx = CHIP_STEPS[i]
        origin = chip_node((2 - dy) % 2, (X - dx) % X) * 2 + core
        return gt.at[pl.ds(origin * 2, 2)]

    def forward_copy(i):
        block = gathered(i) if i < len(CHIP_STEPS) else gt.at[pl.ds(rep * 2, 2)]
        return remote(block, block, fwd_sem.at[0, i], fwd_sem.at[1, i], mate)

    for i in range(len(CHIP_STEPS)):
        gather_copy(i).start()
    forward_copy(len(CHIP_STEPS)).start()

    wself = lax.dot_general(
        x_ref[...], grad_pre, (((0,), (0,)), ((), ())), preferred_element_type=F32
    )
    wneigh = lax.dot_general(
        aggregate, grad_pre, (((0,), (0,)), ((), ())), preferred_element_type=F32
    )
    wbias = jnp.sum(grad_pre.astype(F32), axis=0, keepdims=True)
    for j in range(8):
        wpart[j, 0:16, :] = wself[16 * j : 16 * j + 16, :]
        wpart[j + 8, 0:16, :] = wneigh[16 * j : 16 * j + 16, :]
        wpart[j, 16:24, :] = jnp.broadcast_to(wbias, (8, wbias.shape[1]))
        wpart[j + 8, 16:24, :] = jnp.broadcast_to(wbias, (8, wbias.shape[1]))

    def each_peer(action):
        def body(j, carry):
            action(j)
            return carry

        lax.fori_loop(1, peers, body, 0)

    def w1_copy(j, slot):
        to = lax.rem(rep + j, peers)
        return remote(
            wpart.at[to], win.at[slot], w1_sem.at[0, j], w1_sem.at[1, j], (loop, to)
        )

    def w2_copy(j, slot):
        to = lax.rem(loop + j, peers)
        return remote(
            rows_out.at[to], rows_in.at[slot], w2_sem.at[0, j], w2_sem.at[1, j], (to, rep)
        )

    def w3_copy(j, slot):
        to = lax.rem(loop + j, peers)
        return remote(
            rows_all.at[slot], rows_all.at[slot], w3_sem.at[0, j], w3_sem.at[1, j], (to, rep)
        )

    def w4_copy(j, slot):
        to = lax.rem(rep + j, peers)
        return remote(
            wfull.at[slot], wfull.at[slot], w4_sem.at[0, j], w4_sem.at[1, j], (loop, to)
        )

    each_peer(lambda j: w1_copy(j, rep).start())
    win[rep] = wpart[rep]

    for i in reversed(range(len(CHIP_STEPS))):
        block = gathered(i)
        remote(
            block, block, gath_sem.at[0, i], gath_sem.at[1, i], mate
        ).wait_recv()
        forward_copy(i).start()
    for i in range(len(CHIP_STEPS) + 1):
        if i < len(CHIP_STEPS):
            dy, dx = CHIP_STEPS[i]
            origin = chip_node((2 - dy) % 2, (X - dx) % X) * 2 + (1 - core)
        else:
            origin = chip * 2 + (1 - core)
        block = gt.at[pl.ds(origin * 2, 2)]
        remote(block, block, fwd_sem.at[0, i], fwd_sem.at[1, i], mate).wait_recv()
    for q in range(sources):
        fetch(q).wait()

    def compute(count, k):
        def body(j, carry):
            if k in (0, Z // 2):
                q = loop_node(k, 1 - j)
            else:
                q = loop_node(k * (1 - 2 * (j % 2)), 1 - j // 2)
            live = live_ref[q]
            for t in range(slots):
                d = dst_ref[q, t]
                s = src_ref[q, t]
                on = t < live
                lhs[0:blk, t * blk : (t + 1) * blk] = gt[
                    jnp.where(jnp.logical_and(on, s == 0), d, blocks)
                ]
                lhs[blk : 2 * blk, t * blk : (t + 1) * blk] = gt[
                    jnp.where(jnp.logical_and(on, s == 1), d, blocks)
                ]
            term[j] = jnp.dot(lhs[...], tile_vmem[q], preferred_element_type=F32)
            return carry

        lax.fori_loop(0, count, body, 0)

    def ring_copy(way, col, k):
        src = ring_out.at[way, col, k - 1]
        dst = ring_in.at[way, col, k - 1]
        if k == Z // 2:
            rows = pl.ds(way * blk, blk)
            src, dst = src.at[rows], dst.at[rows]
        return remote(
            src,
            dst,
            ring_sem.at[0, way, col, k - 1],
            ring_sem.at[1, way, col, k - 1],
            (loop_node(1 - 2 * way, 0), rep),
        )

    pending = []

    def launch(copy):
        if pending:
            pending.pop().start()
        if copy is not None:
            pending.append(copy)

    def ring_step(k):
        far = Z // 2
        compute(2 if k == far else 4, k)
        for col in (1, 0):
            for way in (0, 1):
                if k == far:
                    rows = slice(way * blk, (way + 1) * blk)
                    ring_out[way, col, k - 1, rows, :] = term[1 - col, rows, :].astype(BF16)
                else:
                    j = (1 - col) * 2 + way
                    ring_copy(way, col, k + 1).wait_recv()
                    if k == far - 1:
                        rows = slice(way * blk, (way + 1) * blk)
                        rest = slice((1 - way) * blk, (2 - way) * blk)
                        ring_out[way, col, k - 1, rows, :] = (
                            term[j, rows, :] + ring_in[way, col, k, rows, :].astype(F32)
                        ).astype(BF16)
                        ring_out[way, col, k - 1, rest, :] = term[j, rest, :].astype(BF16)
                    else:
                        ring_out[way, col, k - 1] = (
                            term[j] + ring_in[way, col, k].astype(F32)
                        ).astype(BF16)
                launch(ring_copy(way, col, k))
        launch(None)

    ring_step(4)

    each_peer(lambda j: w1_copy(j, lax.rem(rep + peers - j, peers)).wait_recv())
    piece = win[0]
    for j in range(1, peers):
        piece = piece + win[j]
    for m in range(peers):
        rows_out[m, 0:1, :] = piece[m : m + 1, :]
        rows_out[m, 1:2, :] = piece[16:17, :]
    each_peer(lambda j: w2_copy(j, loop).start())
    rows_in[loop] = rows_out[loop]

    ring_step(3)

    each_peer(lambda j: w2_copy(j, lax.rem(loop + peers - j, peers)).wait_recv())
    rows = rows_in[0]
    for j in range(1, peers):
        rows = rows + rows_in[j]
    rows_all[loop] = rows
    grad_scale = 1.0 / math.sqrt(x_ref.shape[0] * peers * peers)
    gb_ref[...] = rows[1:2, :] * grad_scale
    each_peer(lambda j: w3_copy(j, loop).start())

    ring_step(2)

    each_peer(lambda j: w3_copy(j, lax.rem(loop + peers - j, peers)).wait_recv())
    for m in range(peers):
        wfull[rep, m : m + 1, :] = rows_all[m, 0:1, :]
    each_peer(lambda j: w4_copy(j, rep).start())

    ring_step(1)

    compute(2, 0)
    for way in (0, 1):
        ring_copy(way, 1, 1).wait_recv()
    col_out[...] = (
        term[0] + ring_in[0, 1, 0].astype(F32) + ring_in[1, 1, 0].astype(F32)
    ).astype(BF16)
    each_peer(lambda j: w4_copy(j, lax.rem(rep + peers - j, peers)).wait_recv())
    col_copy = remote(col_out, col_in, col_sem.at[0], col_sem.at[1], (loop_node(0, 1), rep))
    col_copy.start()
    for j in range(8):
        gs_ref[16 * j : 16 * j + 16, :] = wfull[j] * grad_scale
        gn_ref[16 * j : 16 * j + 16, :] = wfull[j + 8] * grad_scale
    for way in (0, 1):
        ring_copy(way, 0, 1).wait_recv()
    mine = term[1] + ring_in[0, 0, 0].astype(F32) + ring_in[1, 0, 0].astype(F32)
    col_copy.wait_recv()
    mine = mine + col_in[...].astype(F32)
    for s in range(2):
        rows = slice(s * blk, (s + 1) * blk)
        gin_ref[rows, :] = (self_grad[rows, :] + jnp.transpose(mine[rows, :])).astype(BF16)

    for i in range(len(steps)):
        core_copy(i).wait_send()
        forward_copy(i).wait_send()
    for i in range(len(CHIP_STEPS)):
        chip_copy(i).wait_send()
        gather_copy(i).wait_send()
    for k in range(1, Z // 2 + 1):
        for col in (0, 1):
            for way in (0, 1):
                ring_copy(way, col, k).wait_send()
    col_copy.wait_send()
    each_peer(lambda j: w1_copy(j, rep).wait_send())
    each_peer(lambda j: w2_copy(j, loop).wait_send())
    each_peer(lambda j: w3_copy(j, loop).wait_send())
    each_peer(lambda j: w4_copy(j, rep).wait_send())


def per_device(
    features, w_self, w_neigh, bias, degree, tiles, dst_block, src_block, live_count, cotangent
):
    rows, feat = features.shape
    hidden = w_self.shape[1]
    sources, slots, blk = tiles.shape[2], tiles.shape[3], tiles.shape[4]
    tile_rows = tiles.reshape(sources, slots * blk, blk)
    dst = dst_block[0, 0]
    src = src_block[0, 0]
    live = live_count[0, 0]
    vmem = pl.BlockSpec(memory_space=pltpu.VMEM)
    smem = pl.BlockSpec(memory_space=pltpu.SMEM)
    hbm = pl.BlockSpec(memory_space=pl.ANY)
    dma = pltpu.SemaphoreType.DMA
    shape = jax.ShapeDtypeStruct

    gathered = pl.pallas_call(
        gather_kernel,
        out_shape=shape((sources, rows, feat), BF16),
        in_specs=[vmem],
        out_specs=vmem,
        scratch_shapes=[dma, dma((2,)), dma((2, 2, Z // 2)), dma((2, 2, Z // 2))],
        compiler_params=pltpu.CompilerParams(collective_id=0, has_side_effects=True),
        name="gather_features",
    )(features)

    blocks = 2 * 16
    partial = pl.pallas_call(
        product_kernel,
        out_shape=shape((2, 8, rows, feat), BF16),
        in_specs=[smem, smem, smem, vmem, hbm],
        out_specs=vmem,
        scratch_shapes=[
            pltpu.VMEM((sources, slots * blk, blk), BF16),
            pltpu.VMEM((blocks + 1, blk, feat), F32),
            dma((sources,)),
        ],
        compiler_params=pltpu.CompilerParams(vmem_limit_bytes=40 << 20),
        name="tile_product",
    )(dst, src, live, gathered, tile_rows)

    output, grad_input, grad_self, grad_neigh, grad_bias = pl.pallas_call(
        layer_kernel,
        out_shape=(
            shape((rows, hidden), BF16),
            shape((rows, feat), BF16),
            shape((feat, hidden), F32),
            shape((feat, hidden), F32),
            shape((1, hidden), F32),
        ),
        in_specs=[smem, smem, smem] + [vmem] * 7 + [hbm],
        out_specs=(vmem,) * 5,
        scratch_shapes=[
            pltpu.VMEM((sources, slots * blk, blk), BF16),
            pltpu.VMEM((8, rows, feat), BF16),
            pltpu.VMEM((7, rows, feat), BF16),
            pltpu.VMEM((7, rows, feat), BF16),
            pltpu.VMEM((blocks + 1, feat, blk), BF16),
            pltpu.VMEM((2 * feat, slots * blk), BF16),
            pltpu.VMEM((4, 2 * feat, blk), F32),
            pltpu.VMEM((rows, hidden), F32),
            pltpu.VMEM((rows, feat), F32),
            pltpu.VMEM((2, 2, Z // 2, 2 * feat, blk), BF16),
            pltpu.VMEM((2, 2, Z // 2, 2 * feat, blk), BF16),
            pltpu.VMEM((2 * feat, blk), BF16),
            pltpu.VMEM((2 * feat, blk), BF16),
            pltpu.VMEM((16, 24, hidden), F32),
            pltpu.VMEM((16, 24, hidden), F32),
            pltpu.VMEM((16, 2, hidden), F32),
            pltpu.VMEM((16, 2, hidden), F32),
            pltpu.VMEM((16, 2, hidden), F32),
            pltpu.VMEM((16, 16, hidden), F32),
            dma((sources,)),
            dma((2, 8)),
            dma((2, 7)),
            dma((2, 7)),
            dma((2, 8)),
            dma((2, 2, 2, Z // 2)),
            dma((2,)),
            dma((2, 16)),
            dma((2, 16)),
            dma((2, 16)),
            dma((2, 16)),
        ],
        compiler_params=pltpu.CompilerParams(
            collective_id=1, has_side_effects=True, vmem_limit_bytes=40 << 20
        ),
        name="layer",
    )(
        dst,
        src,
        live,
        partial,
        features,
        w_self,
        w_neigh,
        bias.reshape(1, hidden),
        degree.reshape(rows // blk, blk),
        cotangent,
        tile_rows,
    )
    return output, grad_input, grad_self, grad_neigh, grad_bias.reshape(hidden)


def solution(mesh):
    in_specs = (
        P(("loop", "rep"), None),
        P(),
        P(),
        P(),
        P(("loop", "rep")),
        P("loop", "rep", None, None, None, None),
        P("loop", "rep", None, None),
        P("loop", "rep", None, None),
        P("loop", "rep", None),
        P(("loop", "rep"), None),
    )
    out_specs = (P(("loop", "rep"), None), P(("loop", "rep"), None), P(), P(), P())
    return jax.shard_map(
        per_device, mesh=mesh, in_specs=in_specs, out_specs=out_specs, check_vma=False
    )
```

time: 706 us -> 95.6 us (0.14)
  the two profiles are of different devices: /device:TPU:2 before, /device:TPU:1 now
where the time goes in v1:
time: 95.6 us; the launch traced here: 94.7 us
  Pallas kernels  84.1 us (88%)
  local copies, waits for them, and re-layouts  9.84 us (10%)
    pallas_call x1, Pallas kernels, per_device(): pl.pallas_call(layer_kernel, out_shape=(shape((rows, hidden), BF16), shap...  54.6 us
    pallas_call x1, Pallas kernels, per_device(): pl.pallas_call(gather_kernel, out_shape=shape((sources, rows, feat), BF16...  22.7 us
    unnamed x29, local copies, waits for them, and re-layouts  9.84 us
    pallas_call x1, Pallas kernels, per_device(): pl.pallas_call(product_kernel, out_shape=shape((2, 8, rows, feat), BF16),...  6.75 us

profile of v1, /device:TPU:1, one launch (start us, length us, event | category | flops | bytes accessed | tf_op | source)
XLA Modules:
  0.0 94.7 jit_solution(18214427212257033273)
XLA Ops:
  0.6 0.0 copy-start.3
  0.6 0.0 copy-start.4
  0.7 0.0 copy-start.11
  0.7 0.0 copy-start.10
  0.7 0.0 copy-start.6
  0.7 0.0 copy-start.5
  0.7 22.7 %gather_features.1.g_ref = bf16[16,256,128]{2,1,0:T(8,128)(2,1)} custom-call(bf16[256,128]{1,0:T(8,128)(2,1)} %x_ref.3), custom_call_target="tpu_custom_call" | custom-call | tf_op jit(solution)/shard_map/gather_features/pallas_call | solution.py:531
  23.4 0.0 copy-start
  23.5 3.4 %copy-done = bf16[1,1,16,16,128,128]{5,4,3,2,1,0:T(8,128)(2,1)S(1)} copy-done((bf16[1,1,16,16,128,128]{5,4,3,2,1,0:T(8,128)(2,1)S(1)}, bf16[1,1,16,16,128,128]{5,4,3,2,1,0:T(8,128)(2,1)}, u32[]{:S(2)}) %copy-start) | copy-done | bytes 8388632
  26.8 0.0 copy-start.2
  26.8 1.2 %copy-done.2 = bf16[16,256,128]{2,1,0:T(8,128)(2,1)S(1)} copy-done((bf16[16,256,128]{2,1,0:T(8,128)(2,1)S(1)}, bf16[16,256,128]{2,1,0:T(8,128)(2,1)}, u32[]{:S(2)}) %copy-start.2) | copy-done | bytes 1048600
  28.1 0.0 copy-start.7
  28.1 0.7 copy-done.7
  28.8 0.0 copy-start.8
  28.8 0.7 copy-done.8
  29.5 0.0 copy-start.9
  29.5 0.7 copy-done.9
  30.1 0.0 copy-start.1
  30.1 6.7 %tile_product.1.part_ref = bf16[2,8,256,128]{3,2,1,0:T(8,128)(2,1)S(1)} custom-call(s32[16,16]{1,0:T(8,128)S(1)} %bitcast.9, s32[16,16]{1,0:T(8,128)S(1)} %bitcast.11, s32[16]{0:T(128)S(1)} %bitcast.13, bf16[16,256,128]{2,1,0:T(8,128)(2,1)S(1)} %copy-done.2, bf16[16,2048,128]{2,1,0:T(8,128)(2,1)S(1)} %bitcast.7), custom_call_target="tpu_custom_call" | custom-call | tf_op jit(solution)/shard_map/tile_product/pallas_call | solution.py:542
  36.9 0.0 copy-done.3
  36.9 0.0 copy-done.4
  36.9 0.0 copy-done.11
  36.9 0.0 copy-done.10
  36.9 0.0 copy-done.6
  36.9 0.0 copy-done.5
  36.9 0.0 copy-done.1
  36.9 54.6 %layer.1 = (bf16[256,256]{1,0:T(8,128)(2,1)S(1)}, bf16[256,128]{1,0:T(8,128)(2,1)S(1)}, f32[128,256]{1,0:T(8,128)S(1)}, f32[128,256]{1,0:T(8,128)S(1)}, f32[1,256]{1,0:T(1,128)S(1)}) custom-call(s32[16,16]{1,0:T(8,128)S(1)} %bitcast.10, s32[16,16]{1,0:T(8,128)S(1)} %bitcast.12, s32[16]{0:T(128)S(1)} %bitcast.14, ...), custom_call_target="tpu_custom_call" | custom-call | tf_op jit(solution)/shard_map/layer/pallas_call | solution.py:556
  91.5 0.7 copy.20
  92.2 0.6 copy.21
  92.8 0.7 copy.22
  93.5 0.7 copy.23
  94.1 0.6 copy.24
Async XLA Ops:
  0.6 36.2 %copy-start.3 = (bf16[256,128]{1,0:T(8,128)(2,1)S(1)}, bf16[256,128]{1,0:T(8,128)(2,1)}, u32[]{:S(2)}) copy-start(bf16[256,128]{1,0:T(8,128)(2,1)} %x_ref.3) | copy-start | bytes 196612
  0.6 36.2 %copy-start.4 = (bf16[256,256]{1,0:T(8,128)(2,1)S(1)}, bf16[256,256]{1,0:T(8,128)(2,1)}, u32[]{:S(2)}) copy-start(bf16[256,256]{1,0:T(8,128)(2,1)} %cot_ref.1) | copy-start | bytes 393220
  0.7 36.2 %copy-start.11 = (s32[256]{0:T(256)S(1)}, s32[256]{0:T(256)}, u32[]{:S(2)}) copy-start(s32[256]{0:T(256)} %param.14) | copy-start | bytes 3076
  0.7 36.2 %copy-start.10 = (f32[256]{0:T(256)S(1)}, f32[256]{0:T(256)}, u32[]{:S(2)}) copy-start(f32[256]{0:T(256)} %param.13) | copy-start | bytes 3076
  0.7 36.2 %copy-start.6 = (bf16[128,256]{1,0:T(8,128)(2,1)S(1)}, bf16[128,256]{1,0:T(8,128)(2,1)}, u32[]{:S(2)}) copy-start(bf16[128,256]{1,0:T(8,128)(2,1)} %wn_ref.1) | copy-start | bytes 196612
  0.7 36.2 %copy-start.5 = (bf16[128,256]{1,0:T(8,128)(2,1)S(1)}, bf16[128,256]{1,0:T(8,128)(2,1)}, u32[]{:S(2)}) copy-start(bf16[128,256]{1,0:T(8,128)(2,1)} %ws_ref.1) | copy-start | bytes 196612
  23.4 3.4 %copy-start = (bf16[1,1,16,16,128,128]{5,4,3,2,1,0:T(8,128)(2,1)S(1)}, bf16[1,1,16,16,128,128]{5,4,3,2,1,0:T(8,128)(2,1)}, u32[]{:S(2)}) copy-start(bf16[1,1,16,16,128,128]{5,4,3,2,1,0:T(8,128)(2,1)} %param.15) | copy-start | bytes 25165828
  26.8 1.2 %copy-start.2 = (bf16[16,256,128]{2,1,0:T(8,128)(2,1)S(1)}, bf16[16,256,128]{2,1,0:T(8,128)(2,1)}, u32[]{:S(2)}) copy-start(bf16[16,256,128]{2,1,0:T(8,128)(2,1)} %gather_features.1.g_ref) | copy-start | bytes 3145732
  28.1 0.7 copy-start.7
  28.8 0.7 copy-start.8
  29.5 0.7 copy-start.9
  30.1 6.8 %copy-start.1 = (bf16[1,1,16,16,128,128]{5,4,3,2,1,0:T(8,128)(2,1)S(1)}, bf16[1,1,16,16,128,128]{5,4,3,2,1,0:T(8,128)(2,1)}, u32[]{:S(2)}) copy-start(bf16[1,1,16,16,128,128]{5,4,3,2,1,0:T(8,128)(2,1)} %param.15) | copy-start | bytes 25165828

commit v2 on v1

v2 whole, which is shorter than its diff:
```python
import math

import jax
import jax.numpy as jnp
from jax import lax
from jax.experimental import pallas as pl
from jax.experimental.pallas import tpu as pltpu
from jax.sharding import PartitionSpec as P

F32 = jnp.float32
BF16 = jnp.bfloat16
MESH = pl.DeviceIdType.MESH
Z = 8
X = 4
CHIP_STEPS = ((1, 2), (1, 1), (1, 3), (0, 2), (1, 0), (0, 1), (0, 3))


def remote(src, dst, send_sem, recv_sem, device):
    return pltpu.make_async_remote_copy(
        src_ref=src,
        dst_ref=dst,
        send_sem=send_sem,
        recv_sem=recv_sem,
        device_id=device,
        device_id_type=MESH,
    )


def loop_node(dz, col):
    here = lax.axis_index("loop")
    z = lax.rem(here // 2 + (dz + Z), Z)
    return z * 2 + lax.rem(here % 2 + col, 2)


def chip_node(dy, dx):
    chip = lax.axis_index("rep") // 2
    return lax.rem(chip // X + dy, 2) * X + lax.rem(chip % X + dx, X)


FAR = Z // 2
STRIDE = {1: 1, 2: 2, 3: 1, 4: 2}


def layer_kernel(
    dst_hbm,
    src_hbm,
    live_hbm,
    x_hbm,
    ws_hbm,
    wn_hbm,
    bias_hbm,
    deg_hbm,
    cot_hbm,
    tile_hbm,
    out_ref,
    gin_ref,
    gs_ref,
    gn_ref,
    gb_ref,
    dst_ref,
    src_ref,
    live_ref,
    dst_v,
    live_v,
    x_ref,
    ws_ref,
    wn_ref,
    bias_ref,
    deg_ref,
    cot_ref,
    tile_ref,
    panels,
    here,
    prod,
    run,
    order_v,
    order,
    part,
    core_in,
    chip_out,
    chip_in,
    gt,
    term,
    base,
    self_grad,
    ring_out,
    ring_in,
    col_out,
    col_in,
    wpart,
    win,
    rows_in,
    wmate,
    wfull,
    tile_sem,
    load_sem,
    pair_sem,
    panel_sem,
    core_sem,
    chip_sem,
    gath_sem,
    fwd_sem,
    ring_sem,
    col_sem,
    w1_sem,
    w2_sem,
    w3_sem,
    second_sem,
    third_sem,
):
    loop = lax.axis_index("loop")
    rep = lax.axis_index("rep")
    core = rep % 2
    chip = rep // 2
    mate = (loop, chip * 2 + (1 - core))
    sources, depth, blk = tile_ref.shape
    slots = depth // blk
    total_slots = sources * slots
    blocks = gt.shape[0] - 1
    peers = 16
    left_chip, right_chip, over_chip = chip_node(0, X - 1), chip_node(0, 1), chip_node(1, 0)

    barrier = pltpu.get_barrier_semaphore()

    def greet(semaphore, device):
        pl.semaphore_signal(semaphore, inc=1, device_id=device, device_id_type=MESH)

    for dz, col in ((1, 0), (-1, 0), (2, 0), (-2, 0), (0, 1)):
        greet(barrier, (loop_node(dz, col), rep))
    for other in (left_chip, right_chip, over_chip):
        greet(barrier, (loop, other * 2 + core))
    greet(barrier, mate)

    loads = [
        pltpu.make_async_copy(a, b, load_sem.at[i])
        for i, (a, b) in enumerate(
            (
                (x_hbm, x_ref),
                (dst_hbm, dst_ref),
                (src_hbm, src_ref),
                (live_hbm, live_ref),
                (dst_hbm, dst_v),
                (live_hbm, live_v),
                (ws_hbm, ws_ref),
                (wn_hbm, wn_ref),
                (bias_hbm, bias_ref),
                (deg_hbm, deg_ref),
                (cot_hbm, cot_ref),
            )
        )
    ]
    for copy in loads:
        copy.start()

    def fetch(q):
        return pltpu.make_async_copy(tile_hbm.at[q], tile_ref.at[q], tile_sem.at[q])

    near_first = [(0, 0), (0, 1)]
    for k in range(1, FAR):
        near_first += [(k, 0), (-k, 0), (k, 1), (-k, 1)]
    near_first += [(FAR, 0), (FAR, 1)]
    for dz, col in near_first:
        fetch(loop_node(dz, col)).start()
    loads[0].wait()
    pl.semaphore_wait(barrier, 9)
    def panel(origin, k, s):
        if k == 0:
            return x_ref.at[pl.ds(s * blk, blk)]
        return panels.at[origin * 2 + s]

    def hop(way, col, k, s):
        sign = 1 - 2 * way
        origin = loop_node(0 if k < 3 else -2 * sign, col)
        return remote(
            panel(origin, col if k < 3 else 2, s),
            panels.at[origin * 2 + s],
            panel_sem.at[0, way, col, k - 1, s],
            panel_sem.at[1, way, col, k - 1, s],
            (loop_node(sign * STRIDE[k], 0), rep),
        )

    def arrival(way, col, k, s):
        sign = 1 - 2 * way
        dst = panels.at[loop_node(-sign * k, col) * 2 + s]
        return remote(
            dst,
            dst,
            panel_sem.at[0, way, col, k - 1, s],
            panel_sem.at[1, way, col, k - 1, s],
            (loop_node(sign, 0), rep),
        )

    def pair(s, col):
        rows = pl.ds(s * blk, blk)
        return remote(
            x_ref.at[rows],
            panels.at[loop_node(0, col) * 2 + s],
            pair_sem.at[0, s],
            pair_sem.at[1, s],
            (loop_node(0, 1), rep),
        )

    def on_route(way, k, s):
        return k < FAR or s == way

    for s in range(2):
        pair(s, 0).start()
        for way in (0, 1):
            hop(way, 0, 2, s).start()
    for s in range(2):
        for way in (0, 1):
            hop(way, 0, 1, s).start()
    for other in (left_chip, right_chip):
        greet(second_sem, (loop, other * 2 + core))
    for copy in loads[1:]:
        copy.wait()
    for s in range(2):
        panels[loop * 2 + s] = x_ref[s * blk : (s + 1) * blk, :]
    gt[blocks] = jnp.zeros(gt.shape[1:], BF16)
    run[total_slots] = jnp.zeros(run.shape[1:], BF16)

    def multiply(q):
        fetch(q).wait()
        for s in range(2):
            here[s] = panels[q * 2 + s]
        for t in range(slots):
            prod[q * slots + t] = jnp.dot(
                tile_ref[q, t * blk : (t + 1) * blk, :],
                here[src_ref[q, t]],
                preferred_element_type=F32,
            )

    def multiply_some(nodes):
        count = len(nodes)

        def body(j, carry):
            q = nodes[-1]
            for i in range(count - 1):
                q = jnp.where(j == i, nodes[i], q)
            multiply(q)
            return carry

        lax.fori_loop(0, count, body, 0)

    def sort_slots():
        slot_col = lax.broadcasted_iota(jnp.int32, (sources, slots), 1)
        live_eye = lax.broadcasted_iota(jnp.int32, (sources, sources), 0) == (
            lax.broadcasted_iota(jnp.int32, (sources, sources), 1)
        )
        live_rows = jnp.sum(
            jnp.where(live_eye, jnp.broadcast_to(live_v[...], (sources, sources)), 0),
            axis=1,
            keepdims=True,
        )
        key_grid = jnp.where(slot_col < live_rows, dst_v[...], blocks)
        spread = (
            lax.broadcasted_iota(jnp.int32, (slots, total_slots), 1) % slots
            == lax.broadcasted_iota(jnp.int32, (slots, total_slots), 0)
        )
        pick = (
            lax.broadcasted_iota(jnp.int32, (sources, total_slots), 1) // slots
            == lax.broadcasted_iota(jnp.int32, (sources, total_slots), 0)
        )
        wide = jnp.dot(
            key_grid.astype(F32).astype(BF16),
            spread.astype(F32).astype(BF16),
            preferred_element_type=F32,
        )
        key_row = jnp.sum(jnp.where(pick, wide, 0.0), axis=0, keepdims=True).astype(jnp.int32)
        square = (total_slots, total_slots)
        down = lax.broadcasted_iota(jnp.int32, square, 0)
        across = lax.broadcasted_iota(jnp.int32, square, 1)
        keys = jnp.broadcast_to(key_row, square)
        key_col = jnp.sum(jnp.where(down == across, keys, 0), axis=1, keepdims=True)
        before = jnp.logical_or(
            keys < key_col, jnp.logical_and(keys == key_col, across < down)
        )
        rank = jnp.sum(before.astype(jnp.int32), axis=1, keepdims=True)
        placed = rank == across
        order_v[0:1, :] = jnp.sum(jnp.where(placed, down, 0), axis=0, keepdims=True)
        order_v[1:2, :] = jnp.sum(jnp.where(placed, key_col, 0), axis=0, keepdims=True)
        order_v[2:3, :] = jnp.sum((key_col <= across).astype(jnp.int32), axis=0, keepdims=True)
        order_v[3:4, :] = jnp.sum((key_col == across).astype(jnp.int32), axis=0, keepdims=True)
        order_v[4:8, :] = jnp.zeros((4, total_slots), jnp.int32)
        order_copy().start()

    def order_copy():
        return pltpu.make_async_copy(order_v, order, load_sem.at[11])

    def relay(col):
        for s in range(2):
            for way in (0, 1):
                arrival(way, col, 2, s).wait_recv()
                hop(way, col, 3, s).start()
                if s == way:
                    hop(way, col, 4, s).start()

    def take(k, col):
        for s in range(2):
            for way in (0, 1):
                if on_route(way, k, s):
                    arrival(way, col, k, s).wait_recv()

    def multiply_at(k, col):
        if k in (0, FAR):
            multiply_some([loop_node(k, col)])
        else:
            multiply_some([loop_node(k, col), loop_node(-k, col)])

    multiply_at(0, 0)
    for s in range(2):
        pair(s, 1).wait_recv()
        for way in (0, 1):
            hop(way, 1, 2, s).start()
    for s in range(2):
        for way in (0, 1):
            hop(way, 1, 1, s).start()
    multiply_at(0, 1)
    relay(0)
    take(1, 0)
    multiply_at(1, 0)
    relay(1)
    take(1, 1)
    multiply_at(1, 1)
    base[...] = (
        jnp.dot(x_ref[...], ws_ref[...], preferred_element_type=F32) + bias_ref[...]
    )
    sort_slots()
    pl.semaphore_wait(second_sem, 2)
    for other in (left_chip, right_chip):
        greet(third_sem, (loop, other * 2 + core))
    for col in (0, 1):
        multiply_at(2, col)
    for col in (0, 1):
        take(3, col)
        multiply_at(3, col)
        take(4, col)
        multiply_at(4, col)
    order_copy().wait()
    pl.semaphore_wait(third_sem, 2)

    def accumulate(i, total):
        for u in range(8):
            j = i * 8 + u
            same = jnp.logical_and(j > 0, order[1, j] == order[1, jnp.maximum(j - 1, 0)])
            total = total * jnp.where(same, 1.0, 0.0) + prod[order[0, j]]
            run[j] = total.astype(BF16)
        return total

    lax.fori_loop(0, total_slots // 8, accumulate, jnp.zeros((blk, blk), F32))

    steps = CHIP_STEPS + ((0, 0),)

    def collect(side, i):
        for s in range(2):
            which = core if side == 0 else 1 - core
            d = (chip_node(*steps[i]) * 2 + which) * 2 + s
            part[side, i, s * blk : (s + 1) * blk, :] = run[
                jnp.where(order[3, d] > 0, order[2, d] - 1, total_slots)
            ]

    def core_copy(i):
        return remote(
            part.at[1, i], core_in.at[i], core_sem.at[0, i], core_sem.at[1, i], mate
        )

    def chip_copy(i):
        return remote(
            chip_out.at[i],
            chip_in.at[i],
            chip_sem.at[0, i],
            chip_sem.at[1, i],
            (loop, chip_node(*steps[i]) * 2 + core),
        )

    for i in range(len(steps)):
        collect(1, i)
        if i > 0:
            core_copy(i - 1).start()
    last = len(steps) - 1
    collect(0, 0)
    core_copy(last).start()
    for i in range(last):
        collect(0, i + 1)
        core_copy(i).wait_recv()
        both = part[0, i].astype(F32) + core_in[i].astype(F32)
        chip_out[i] = both.astype(BF16)
        if i > 0:
            chip_copy(i - 1).start()
    core_copy(last).wait_recv()
    total = part[0, last].astype(F32) + core_in[last].astype(F32)
    chip_copy(last - 1).start()
    for i in reversed(range(last)):
        chip_copy(i).wait_recv()
        total = total + chip_in[i].astype(F32)

    deg_rows = deg_ref[...].astype(F32)
    deg_cols = jnp.concatenate(
        [
            jnp.transpose(jnp.broadcast_to(deg_rows[s : s + 1, :], (blk, blk)))
            for s in range(2)
        ],
        axis=0,
    )
    aggregate = (total / deg_cols).astype(BF16)
    preact = base[...] + jnp.dot(aggregate, wn_ref[...], preferred_element_type=F32)
    sigmoid_val = jax.nn.sigmoid(preact)
    grad_pre = (
        cot_ref[...].astype(F32) * sigmoid_val * (1.0 + preact * (1.0 - sigmoid_val))
    ).astype(BF16)
    out_ref[...] = (preact * sigmoid_val).astype(BF16)
    back = lax.dot_general(
        wn_ref[...], grad_pre, (((1,), (1,)), ((), ())), preferred_element_type=F32
    )
    for s in range(2):
        gt[rep * 2 + s] = (back[:, s * blk : (s + 1) * blk] / deg_rows[s : s + 1, :]).astype(BF16)
    self_grad[...] = lax.dot_general(
        grad_pre, ws_ref[...], (((1,), (1,)), ((), ())), preferred_element_type=F32
    )

    def gather_copy(i):
        dy, dx = CHIP_STEPS[i]
        mine = gt.at[pl.ds(rep * 2, 2)]
        return remote(
            mine,
            mine,
            gath_sem.at[0, i],
            gath_sem.at[1, i],
            (loop, chip_node(dy, dx) * 2 + core),
        )

    def gathered(i):
        dy, dx = CHIP_STEPS[i]
        origin = chip_node((2 - dy) % 2, (X - dx) % X) * 2 + core
        return gt.at[pl.ds(origin * 2, 2)]

    def forward_copy(i):
        block = gathered(i) if i < len(CHIP_STEPS) else gt.at[pl.ds(rep * 2, 2)]
        return remote(block, block, fwd_sem.at[0, i], fwd_sem.at[1, i], mate)

    for i in range(len(CHIP_STEPS)):
        gather_copy(i).start()
    forward_copy(len(CHIP_STEPS)).start()

    wself = lax.dot_general(
        x_ref[...], grad_pre, (((0,), (0,)), ((), ())), preferred_element_type=F32
    )
    wneigh = lax.dot_general(
        aggregate, grad_pre, (((0,), (0,)), ((), ())), preferred_element_type=F32
    )
    wbias = jnp.sum(grad_pre.astype(F32), axis=0, keepdims=True)
    for j in range(8):
        wpart[j, 0:16, :] = wself[16 * j : 16 * j + 16, :]
        wpart[j + 8, 0:16, :] = wneigh[16 * j : 16 * j + 16, :]
        wpart[j, 16:24, :] = jnp.broadcast_to(wbias, (8, wbias.shape[1]))
        wpart[j + 8, 16:24, :] = jnp.broadcast_to(wbias, (8, wbias.shape[1]))
    piece = core * 8 + chip

    def w1_mate():
        return remote(
            wpart.at[pl.ds((1 - core) * 8, 8)], wmate, w1_sem.at[0, 7], w1_sem.at[1, 7], mate
        )

    def w1_copy(i, sending):
        dy, dx = CHIP_STEPS[i]
        slot = chip if sending else chip_node((2 - dy) % 2, (X - dx) % X)
        to = chip_node(dy, dx)
        return remote(
            wpart.at[core * 8 + to],
            win.at[slot],
            w1_sem.at[0, i],
            w1_sem.at[1, i],
            (loop, to * 2 + core),
        )

    def w2_copy(stage, j, sending):
        step = 4**stage
        own = loop // step % 4
        to = loop + (lax.rem(own + j, 4) - own) * step
        slot = own if sending else lax.rem(own + 4 - j, 4)
        block = rows_in.at[stage, slot]
        return remote(
            block, block, w2_sem.at[0, stage, j], w2_sem.at[1, stage, j], (to, rep)
        )

    def w2_send(stage, value):
        rows_in[stage, loop // 4**stage % 4] = value
        for j in range(1, 4):
            pending.append(w2_copy(stage, j, True))

    def w2_sum(stage):
        for j in range(1, 4):
            w2_copy(stage, j, False).wait_recv()
        value = rows_in[stage, 0]
        for j in range(1, 4):
            value = value + rows_in[stage, j]
        return value

    def w3_copy(i, sending):
        dy, dx = CHIP_STEPS[i]
        slot = chip if sending else chip_node((2 - dy) % 2, (X - dx) % X)
        block = wfull.at[core * 8 + slot]
        return remote(
            block,
            block,
            w3_sem.at[0, i],
            w3_sem.at[1, i],
            (loop, chip_node(dy, dx) * 2 + core),
        )

    def w3_mate(side):
        block = wfull.at[pl.ds(side * 8, 8)]
        return remote(block, block, w3_sem.at[0, 7], w3_sem.at[1, 7], mate)

    w1_mate().start()
    for i in reversed(range(len(CHIP_STEPS))):
        block = gathered(i)
        remote(
            block, block, gath_sem.at[0, i], gath_sem.at[1, i], mate
        ).wait_recv()
        forward_copy(i).start()
        if i == 4:
            w1_mate().wait_recv()
            for j in range(8):
                wpart[core * 8 + j] = wpart[core * 8 + j] + wmate[j]
            win[chip] = wpart[piece]
        if i == 3:
            for j in range(len(CHIP_STEPS)):
                w1_copy(j, True).start()
    for i in range(len(CHIP_STEPS) + 1):
        if i < len(CHIP_STEPS):
            dy, dx = CHIP_STEPS[i]
            origin = chip_node((2 - dy) % 2, (X - dx) % X) * 2 + (1 - core)
        else:
            origin = chip * 2 + (1 - core)
        block = gt.at[pl.ds(origin * 2, 2)]
        remote(block, block, fwd_sem.at[0, i], fwd_sem.at[1, i], mate).wait_recv()

    def compute(count, k, first):
        def body(j, carry):
            if k in (0, FAR):
                q = loop_node(k, 1 - j)
            else:
                q = loop_node(k * (1 - 2 * (j % 2)), 1 - j // 2)
            sums = [jnp.zeros((blk, blk), F32) for _ in range(2)]
            for t in range(slots):
                d = jnp.where(t < live_ref[0, q], dst_ref[q, t], blocks)
                value = jnp.dot(
                    gt[d], tile_ref[q, t * blk : (t + 1) * blk, :], preferred_element_type=F32
                )
                for s in range(2):
                    sums[s] = sums[s] + value * jnp.where(src_ref[q, t] == s, 1.0, 0.0)
            for s in range(2):
                term[first + j, s * blk : (s + 1) * blk, :] = sums[s]
            return carry

        lax.fori_loop(0, count, body, 0)

    def ring_copy(way, col, k, s):
        rows = pl.ds(s * blk, blk)
        return remote(
            ring_out.at[way, col, k - 1, rows],
            ring_in.at[way, col, k - 1, rows],
            ring_sem.at[0, way, col, k - 1, s],
            ring_sem.at[1, way, col, k - 1, s],
            (loop_node((1 - 2 * way) * STRIDE[k], 0), rep),
        )

    pending = []

    def launch(copy):
        while pending:
            pending.pop(0).start()
        if copy is not None:
            pending.append(copy)

    def ring_send(k, first, cols):
        for col in cols:
            for s in range(2):
                rows = slice(s * blk, (s + 1) * blk)
                for way in (0, 1):
                    if not on_route(way, k, s):
                        continue
                    j = first + (1 - col if k == FAR else (1 - col) * 2 + way)
                    value = term[j, rows, :]
                    if k == 2:
                        ring_copy(way, col, 3, s).wait_recv()
                        value = value + ring_in[way, col, 2, rows, :].astype(F32)
                        if s == way:
                            ring_copy(way, col, 4, s).wait_recv()
                            value = value + ring_in[way, col, 3, rows, :].astype(F32)
                    ring_out[way, col, k - 1, rows, :] = value.astype(BF16)
                    launch(ring_copy(way, col, k, s))

    compute(4, 3, 0)
    ring_send(3, 0, (1, 0))
    compute(2, FAR, 4)
    ring_send(FAR, 4, (1, 0))
    launch(None)
    compute(4, 2, 0)
    for i in reversed(range(len(CHIP_STEPS))):
        w1_copy(i, False).wait_recv()
    value = win[0]
    for j in range(1, 8):
        value = value + win[j]
    w2_send(0, value)
    compute(4, 1, 4)
    ring_send(1, 4, (1, 0))
    ring_send(2, 0, (1,))
    w2_send(1, w2_sum(0))
    ring_send(2, 0, (0,))
    launch(None)
    compute(2, 0, 0)
    grad_scale = 1.0 / math.sqrt(x_ref.shape[0] * peers * peers)
    value = w2_sum(1)
    gb_ref[...] = value[16:17, :] * grad_scale
    wfull[piece] = value[0:16, :] * grad_scale

    def arrived(col, s):
        rows = slice(s * blk, (s + 1) * blk)
        value = term[1 - col, rows, :]
        for way in (0, 1):
            for k in (1, 2):
                ring_copy(way, col, k, s).wait_recv()
                value = value + ring_in[way, col, k - 1, rows, :].astype(F32)
        return value

    def col_copy(s):
        rows = pl.ds(s * blk, blk)
        return remote(
            col_out.at[rows],
            col_in.at[rows],
            col_sem.at[0, s],
            col_sem.at[1, s],
            (loop_node(0, 1), rep),
        )

    for s in range(2):
        col_out[s * blk : (s + 1) * blk, :] = arrived(1, s).astype(BF16)
        if s == 0:
            for i in range(len(CHIP_STEPS)):
                w3_copy(i, True).start()
        else:
            col_copy(0).start()
    mine = [arrived(0, 0)]
    col_copy(1).start()
    mine.append(arrived(0, 1))
    for i in reversed(range(len(CHIP_STEPS))):
        w3_copy(i, False).wait_recv()
    w3_mate(core).start()
    for s in range(2):
        rows = slice(s * blk, (s + 1) * blk)
        col_copy(s).wait_recv()
        value = mine[s] + col_in[rows, :].astype(F32)
        gin_ref[rows, :] = (self_grad[rows, :] + jnp.transpose(value)).astype(BF16)
    w3_mate(1 - core).wait_recv()
    for j in range(8):
        gs_ref[16 * j : 16 * j + 16, :] = wfull[j]
        gn_ref[16 * j : 16 * j + 16, :] = wfull[j + 8]

    for s in range(2):
        pair(s, 0).wait_send()
        col_copy(s).wait_send()
    for i in range(len(steps)):
        core_copy(i).wait_send()
        forward_copy(i).wait_send()
    for i in range(len(CHIP_STEPS)):
        chip_copy(i).wait_send()
        gather_copy(i).wait_send()
    for k in range(1, FAR + 1):
        for col in (0, 1):
            for s in range(2):
                for way in (0, 1):
                    if on_route(way, k, s):
                        hop(way, col, k, s).wait_send()
                        ring_copy(way, col, k, s).wait_send()
    for i in range(len(CHIP_STEPS)):
        w1_copy(i, True).wait_send()
        w3_copy(i, True).wait_send()
    for stage in range(2):
        for j in range(1, 4):
            w2_copy(stage, j, True).wait_send()
    w1_mate().wait_send()
    w3_mate(core).wait_send()


def finish_kernel(*refs):
    for a, b in zip(refs[:5], refs[5:]):
        b[...] = a[...]


def per_device(
    features, w_self, w_neigh, bias, degree, tiles, dst_block, src_block, live_count, cotangent
):
    rows, feat = features.shape
    hidden = w_self.shape[1]
    sources, slots, blk = tiles.shape[2], tiles.shape[3], tiles.shape[4]
    blocks = 2 * 16
    vmem = pl.BlockSpec(memory_space=pltpu.VMEM)
    hbm = pl.BlockSpec(memory_space=pl.ANY)
    dma = pltpu.SemaphoreType.DMA
    shape = jax.ShapeDtypeStruct
    smem = pltpu.SMEM

    results = (
        shape((rows, hidden), BF16),
        shape((rows, feat), BF16),
        shape((feat, hidden), F32),
        shape((feat, hidden), F32),
        shape((1, hidden), F32),
    )
    made = pl.pallas_call(
        layer_kernel,
        out_shape=results,
        in_specs=[hbm] * 10,
        out_specs=(vmem,) * 5,
        scratch_shapes=[
            smem((sources, slots), jnp.int32),
            smem((sources, slots), jnp.int32),
            smem((1, sources), jnp.int32),
            pltpu.VMEM((sources, slots), jnp.int32),
            pltpu.VMEM((1, sources), jnp.int32),
            pltpu.VMEM((rows, feat), BF16),
            pltpu.VMEM((feat, hidden), BF16),
            pltpu.VMEM((feat, hidden), BF16),
            pltpu.VMEM((1, hidden), F32),
            pltpu.VMEM((rows // blk, blk), jnp.int32),
            pltpu.VMEM((rows, hidden), BF16),
            pltpu.VMEM((sources, slots * blk, blk), BF16),
            pltpu.VMEM((sources * 2, blk, feat), BF16),
            pltpu.VMEM((2, blk, feat), BF16),
            pltpu.VMEM((sources * slots, blk, feat), F32),
            pltpu.VMEM((sources * slots + 1, blk, feat), BF16),
            pltpu.VMEM((8, sources * slots), jnp.int32),
            smem((8, sources * slots), jnp.int32),
            pltpu.VMEM((2, 8, rows, feat), BF16),
            pltpu.VMEM((8, rows, feat), BF16),
            pltpu.VMEM((7, rows, feat), BF16),
            pltpu.VMEM((7, rows, feat), BF16),
            pltpu.VMEM((blocks + 1, feat, blk), BF16),
            pltpu.VMEM((8, 2 * feat, blk), F32),
            pltpu.VMEM((rows, hidden), F32),
            pltpu.VMEM((rows, feat), F32),
            pltpu.VMEM((2, 2, FAR, 2 * feat, blk), BF16),
            pltpu.VMEM((2, 2, FAR, 2 * feat, blk), BF16),
            pltpu.VMEM((2 * feat, blk), BF16),
            pltpu.VMEM((2 * feat, blk), BF16),
            pltpu.VMEM((16, 24, hidden), F32),
            pltpu.VMEM((8, 24, hidden), F32),
            pltpu.VMEM((2, 4, 24, hidden), F32),
            pltpu.VMEM((8, 24, hidden), F32),
            pltpu.VMEM((16, 16, hidden), F32),
            dma((sources,)),
            dma((12,)),
            dma((2, 2)),
            dma((2, 2, 2, FAR, 2)),
            dma((2, 8)),
            dma((2, 7)),
            dma((2, 7)),
            dma((2, 8)),
            dma((2, 2, 2, FAR, 2)),
            dma((2, 2)),
            dma((2, 8)),
            dma((2, 2, 4)),
            dma((2, 8)),
            pltpu.SemaphoreType.REGULAR,
            pltpu.SemaphoreType.REGULAR,
        ],
        compiler_params=pltpu.CompilerParams(
            collective_id=0, has_side_effects=True, vmem_limit_bytes=57 << 20
        ),
        name="layer",
    )(
        dst_block.reshape(sources, slots),
        src_block.reshape(sources, slots),
        live_count.reshape(1, sources),
        features,
        w_self,
        w_neigh,
        bias.reshape(1, hidden),
        degree.reshape(rows // blk, blk),
        cotangent,
        tiles.reshape(sources, slots * blk, blk),
    )
    output, grad_input, grad_self, grad_neigh, grad_bias = pl.pallas_call(
        finish_kernel,
        out_shape=results,
        in_specs=[vmem] * 5,
        out_specs=(vmem,) * 5,
        name="finish",
    )(*made)
    return output, grad_input, grad_self, grad_neigh, grad_bias.reshape(hidden)


def solution(mesh):
    in_specs = (
        P(("loop", "rep"), None),
        P(),
        P(),
        P(),
        P(("loop", "rep")),
        P("loop", "rep", None, None, None, None),
        P("loop", "rep", None, None),
        P("loop", "rep", None, None),
        P("loop", "rep", None),
        P(("loop", "rep"), None),
    )
    out_specs = (P(("loop", "rep"), None), P(("loop", "rep"), None), P(), P(), P())
    return jax.shard_map(
        per_device, mesh=mesh, in_specs=in_specs, out_specs=out_specs, check_vma=False
    )
```

time: 95.6 us -> 81.2 us (0.85)
  local copies, waits for them, and re-layouts: 9.84 us -> 0 us
  Pallas kernels: 84.1 us -> 80.4 us
    unnamed x29 -> x0, local copies, waits for them, and re-layouts: 9.84 us -> none
    pallas_call x3 -> x2, Pallas kernels: 84.1 us -> 80.4 us  [the longest x1 78.6 us: per_device(): pl.pallas_call(layer_kernel, out_shape=results, in_specs=[hbm] * 10, out_...]
where the time goes in v2:
time: 81.2 us; the launch traced here: 81.1 us
  Pallas kernels  80.4 us (99%)
    pallas_call x1, Pallas kernels, per_device(): pl.pallas_call(layer_kernel, out_shape=results, in_specs=[hbm] * 10, out_...  78.6 us
    pallas_call x1, Pallas kernels, per_device(): pl.pallas_call(finish_kernel, out_shape=results, in_specs=[vmem] * 5, out...  1.84 us

profile of v2, /device:TPU:1, one launch (start us, length us, event | category | flops | bytes accessed | tf_op | source)
XLA Modules:
  0.0 81.1 jit_solution(4846973054360825391)
XLA Ops:
  0.6 78.6 %layer.1 = (bf16[256,256]{1,0:T(8,128)(2,1)}, bf16[256,128]{1,0:T(8,128)(2,1)}, f32[128,256]{1,0:T(8,128)}, f32[128,256]{1,0:T(8,128)}, f32[1,256]{1,0:T(1,128)}) custom-call(s32[16,16]{1,0:T(8,128)} %bitcast.8, s32[16,16]{1,0:T(8,128)} %bitcast.9, s32[1,16]{1,0:T(1,128)} %bitcast.12, bf16[256,128]{1,0:T(8,128)(2,1)} %x_hbm.1, bf16[128,256]{1,0:T(8,128)(2,1)} %ws_hbm.1, ...), custom_call_target="tpu_custom_call" | custom-call | tf_op jit(solution)/shard_map/layer/pallas_call | solution.py:712
  79.2 1.8 %finish.1 = (bf16[256,256]{1,0:T(8,128)(2,1)}, bf16[256,128]{1,0:T(8,128)(2,1)}, f32[128,256]{1,0:T(8,128)}, f32[128,256]{1,0:T(8,128)}, f32[1,256]{1,0:T(1,128)}) custom-call(bf16[256,256]{1,0:T(8,128)(2,1)} %get-tuple-element.15.refs_0_, bf16[256,128]{1,0:T(8,128)(2,1)} %get-tuple-element.16.refs_1_, f32[128,256]{1,0:T(8,128)} %get-tuple-element.17.refs_2_, ...), custom_call_target="tpu_custom_call" | custom-call | tf_op jit(solution)/shard_map/finish/pallas_call | solution.py:785

commit v3 on v2

--- a/solution.py
+++ b/solution.py
@@ -170,6 +170,15 @@
 
     def hop(way, col, k, s):
         sign = 1 - 2 * way
+        if col == 1 and k > 1:
+            block = panels.at[loop_node(-sign * k, 0) * 2 + s]
+            return remote(
+                block,
+                block,
+                panel_sem.at[0, way, col, k - 1, s],
+                panel_sem.at[1, way, col, k - 1, s],
+                (loop_node(0, 1), rep),
+            )
         origin = loop_node(0 if k < 3 else -2 * sign, col)
         return remote(
             panel(origin, col if k < 3 else 2, s),
@@ -287,13 +296,17 @@
     def order_copy():
         return pltpu.make_async_copy(order_v, order, load_sem.at[11])
 
-    def relay(col):
+    def relay(k):
         for s in range(2):
             for way in (0, 1):
-                arrival(way, col, 2, s).wait_recv()
-                hop(way, col, 3, s).start()
-                if s == way:
-                    hop(way, col, 4, s).start()
+                if not on_route(way, k, s):
+                    continue
+                arrival(way, 0, k, s).wait_recv()
+                if k == 2:
+                    hop(way, 0, 3, s).start()
+                    if s == way:
+                        hop(way, 0, 4, s).start()
+                hop(way, 1, k, s).start()
 
     def take(k, col):
         for s in range(2):
@@ -311,17 +324,15 @@
     for s in range(2):
         pair(s, 1).wait_recv()
         for way in (0, 1):
-            hop(way, 1, 2, s).start()
-    for s in range(2):
-        for way in (0, 1):
             hop(way, 1, 1, s).start()
+    relay(2)
     multiply_at(0, 1)
-    relay(0)
     take(1, 0)
     multiply_at(1, 0)
-    relay(1)
     take(1, 1)
     multiply_at(1, 1)
+    relay(3)
+    relay(4)
     base[...] = (
         jnp.dot(x_ref[...], ws_ref[...], preferred_element_type=F32) + bias_ref[...]
     )
@@ -329,13 +340,12 @@
     pl.semaphore_wait(second_sem, 2)
     for other in (left_chip, right_chip):
         greet(third_sem, (loop, other * 2 + core))
-    for col in (0, 1):
-        multiply_at(2, col)
-    for col in (0, 1):
-        take(3, col)
-        multiply_at(3, col)
-        take(4, col)
-        multiply_at(4, col)
+    multiply_at(2, 0)
+    multiply_at(3, 0)
+    multiply_at(4, 0)
+    for k in (2, 3, 4):
+        take(k, 1)
+        multiply_at(k, 1)
     order_copy().wait()
     pl.semaphore_wait(third_sem, 2)
 
@@ -594,27 +604,30 @@
 
     compute(4, 3, 0)
     ring_send(3, 0, (1, 0))
-    compute(2, FAR, 4)
-    ring_send(FAR, 4, (1, 0))
-    launch(None)
-    compute(4, 2, 0)
     for i in reversed(range(len(CHIP_STEPS))):
         w1_copy(i, False).wait_recv()
     value = win[0]
     for j in range(1, 8):
         value = value + win[j]
     w2_send(0, value)
+    compute(2, FAR, 4)
+    ring_send(FAR, 4, (1, 0))
+    launch(None)
+    compute(4, 2, 0)
     compute(4, 1, 4)
-    ring_send(1, 4, (1, 0))
+    w2_send(1, w2_sum(0))
+    ring_send(1, 4, (1,))
     ring_send(2, 0, (1,))
-    w2_send(1, w2_sum(0))
+    ring_send(1, 4, (0,))
     ring_send(2, 0, (0,))
     launch(None)
-    compute(2, 0, 0)
     grad_scale = 1.0 / math.sqrt(x_ref.shape[0] * peers * peers)
     value = w2_sum(1)
     gb_ref[...] = value[16:17, :] * grad_scale
     wfull[piece] = value[0:16, :] * grad_scale
+    compute(2, 0, 0)
+    for i in range(len(CHIP_STEPS)):
+        w3_copy(i, True).start()
 
     def arrived(col, s):
         rows = slice(s * blk, (s + 1) * blk)
@@ -637,10 +650,7 @@
 
     for s in range(2):
         col_out[s * blk : (s + 1) * blk, :] = arrived(1, s).astype(BF16)
-        if s == 0:
-            for i in range(len(CHIP_STEPS)):
-                w3_copy(i, True).start()
-        else:
+        if s == 1:
             col_copy(0).start()
     mine = [arrived(0, 0)]
     col_copy(1).start()

time: 81.2 us -> 75.1 us (0.925)
  Pallas kernels: 80.4 us -> 74.2 us
    pallas_call x1, Pallas kernels: 78.6 us -> 72.3 us  [per_device(): pl.pallas_call(layer_kernel, out_shape=results, in_specs=[hbm] * 10, out_...]
where the time goes in v3:
time: 75.1 us; the launch traced here: 74.8 us
  Pallas kernels  74.2 us (99%)
    pallas_call x1, Pallas kernels, per_device(): pl.pallas_call(layer_kernel, out_shape=results, in_specs=[hbm] * 10, out_...  72.3 us
    pallas_call x1, Pallas kernels, per_device(): pl.pallas_call(finish_kernel, out_shape=results, in_specs=[vmem] * 5, out...  1.84 us

profile of v3, /device:TPU:1, one launch (start us, length us, event | category | flops | bytes accessed | tf_op | source)
XLA Modules:
  0.0 74.8 jit_solution(17421093684449985413)
XLA Ops:
  0.6 72.3 %layer.1 = (bf16[256,256]{1,0:T(8,128)(2,1)}, bf16[256,128]{1,0:T(8,128)(2,1)}, f32[128,256]{1,0:T(8,128)}, f32[128,256]{1,0:T(8,128)}, f32[1,256]{1,0:T(1,128)}) custom-call(s32[16,16]{1,0:T(8,128)} %bitcast.8, s32[16,16]{1,0:T(8,128)} %bitcast.9, s32[1,16]{1,0:T(1,128)} %bitcast.12, bf16[256,128]{1,0:T(8,128)(2,1)} %x_hbm.1, bf16[128,256]{1,0:T(8,128)(2,1)} %ws_hbm.1, ...), custom_call_target="tpu_custom_call" | custom-call | tf_op jit(solution)/shard_map/layer/pallas_call | solution.py:722
  73.0 1.8 %finish.1 = (bf16[256,256]{1,0:T(8,128)(2,1)}, bf16[256,128]{1,0:T(8,128)(2,1)}, f32[128,256]{1,0:T(8,128)}, f32[128,256]{1,0:T(8,128)}, f32[1,256]{1,0:T(1,128)}) custom-call(bf16[256,256]{1,0:T(8,128)(2,1)} %get-tuple-element.15.refs_0_, bf16[256,128]{1,0:T(8,128)(2,1)} %get-tuple-element.16.refs_1_, f32[128,256]{1,0:T(8,128)} %get-tuple-element.17.refs_2_, ...), custom_call_target="tpu_custom_call" | custom-call | tf_op jit(solution)/shard_map/finish/pallas_call | solution.py:795
